TPU v7x, 128 devices: a whole 4x4x4 slice. The times are simulated.
128 devices in a mesh: row: 16 (over x, z), col: 8 (over y, core).
Axes of the slice: x: 4, y: 4, z: 4, core: 2. Of those that a mesh axis runs over, the one named last changes fastest.
Arguments:
- primal_rows: bfloat16 [16384, 8192], P('row', 'col'), may hold values from -6 to 6
- dual_rows: bfloat16 [16384, 8192], P('row', 'col'), may hold values from -6 to 6
- weight_rows: bfloat16 [16384, 8192], P('row', 'col'), may hold values from -0.0625 to 0.0625
- pairs: int32 [384, 2], P('row'), may hold values from 0 to 63, as said below
Outputs:
- tiles: float32 [384, 256, 256], P('row', 'col')
Inputs may be any that keep to these rules, and one draw needn't show every extreme that they name: `pairs`: tile rows r * 24 to (r + 1) * 24 - 1 have their first block i among blocks r * 4 to (r + 1) * 4 - 1. Among their second blocks j, the blocks held by any other row index q (blocks q * 4 to (q + 1) * 4 - 1) are exactly one block, named one or more times; blocks of r itself may appear too.
All inputs are finite; a program needn't handle non-finite values.
Results may differ from a plain program's by a relative error of at most 0.0003.
Values may be sent and summed in bfloat16 or wider, within the bound.
No kernel may reach another device: no remote copies, remote signals or barrier semaphores. Data moves between devices by JAX's collectives and lax.ppermute only.
A program may use at most 128 MiB of HBM per device.

v0:
```python
import jax
import jax.numpy as jnp
from jax import lax
from jax.sharding import PartitionSpec as P

TILE = 256


def shards(primal_rows, dual_rows, weight_rows, pairs):
    row_count = lax.axis_size("row")
    my_row = lax.axis_index("row")
    per_row = primal_rows.shape[0] // TILE
    features = primal_rows.shape[1]
    tile_count = pairs.shape[0]
    every_pair = lax.all_gather(pairs, "row", axis=0, tiled=True)
    wanted = every_pair.reshape(row_count, tile_count * 2)
    held_here = wanted // per_row == my_row
    local_pick = jnp.max(jnp.where(held_here, wanted - my_row * per_row, 0), axis=1)
    weight_blocks = weight_rows.reshape(per_row, TILE, features)
    outgoing = jnp.take(weight_blocks, local_pick, axis=0)
    incoming = lax.all_to_all(outgoing, "row", split_axis=0, concat_axis=0, tiled=True)
    block_table = jnp.concatenate([weight_blocks, incoming], axis=0)
    first_local = pairs[:, 0] - my_row * per_row
    second_block = pairs[:, 1]
    second_row = second_block // per_row
    second_slot = jnp.where(
        second_row == my_row, second_block - my_row * per_row, per_row + second_row
    )
    left_x = jnp.take(primal_rows.reshape(per_row, TILE, features), first_local, axis=0)
    left_s = jnp.take(dual_rows.reshape(per_row, TILE, features), first_local, axis=0)
    right_rows = jnp.take(block_table, second_slot, axis=0)
    cross_x = jnp.einsum("tak,tbk->tab", left_x, right_rows, preferred_element_type=jnp.float32)
    cross_s = jnp.einsum("tak,tbk->tab", left_s, right_rows, preferred_element_type=jnp.float32)
    stacked = jnp.stack([cross_x, cross_s])
    whole = lax.psum(stacked, "col")
    slice_rows = TILE // lax.axis_size("col")
    summed = lax.dynamic_slice_in_dim(whole, lax.axis_index("col") * slice_rows, slice_rows, 2)
    return summed[0] * summed[1]


def solution(mesh):
    placed = (P("row", "col"), P("row", "col"), P("row", "col"), P("row", None))
    return jax.shard_map(
        shards, mesh=mesh, in_specs=placed, out_specs=P("row", "col", None), check_vma=False
    )
```

profile of v0, /device:TPU:1, one launch (start us, length us, event | category | flops | bytes accessed | tf_op | source)
XLA Modules:
  0.0 358.9 jit_solution(2798819045864562003)
XLA Ops:
  6.5 0.0 copy-start
  6.5 20.3 %all-gather = s32[16,24,2]{1,2,0:T(2,128)S(1)} all-gather(s32[1,24,2]{1,2,0:T(2,128)} %bitcast.26), channel_id=1, replica_groups=mesh['row'=16,'col'=8] {'row'}, dimensions={0}, use_global_device_ids=true | all-gather | bytes 3264 | tf_op jit(solution)/shard_map/all_gather | solution.py:15
  26.8 0.1 reshape.79
  27.0 0.1 reduce_max.15
  27.0 0.1 reduce_max.20
  27.2 6.2 %gather_fusion = bf16[16,256,1024]{2,1,0:T(8,128)(2,1)} fusion(bf16[4,256,1024]{2,1,0:T(8,128)(2,1)} %bitcast.24, s32[1024]{0:T(1024)S(1)} %pad_clamp_fusion.1), kind=kCustom, calls=%fused_computation.2 | custom fusion | bytes 16777280 | tf_op jit(solution)/shard_map/jit(_take)/gather | solution.py:20
  33.4 7.4 %broadcast_select_fusion.1 = bf16[16,256,1024]{2,1,0:T(8,128)(2,1)} fusion(bf16[16,256,1024]{2,1,0:T(8,128)(2,1)} %gather_fusion, pred[16]{0:T(512)(128)(4,1)S(1)} %compare_and_fusion.1), kind=kLoop, calls=%fused_computation.13 | loop fusion | flops 4194304 | bytes 16777232 | tf_op jit(solution)/shard_map/jit(_take)/select_n | solution.py:20
  40.9 4.9 %all-to-all-start = ((bf16[16,256,1024]{2,1,0:T(8,128)(2,1)}), bf16[16,256,1024]{2,1,0:T(8,128)(2,1)}, u32[]{:S(2)}, u32[]{:S(2)}) async-start(bf16[16,256,1024]{2,1,0:T(8,128)(2,1)} %broadcast_select_fusion.1), calls=%async_computation | async-start | bytes 16777216 | tf_op jit(solution)/shard_map/all_to_all | solution.py:21
  45.8 0.0 all-reduce.2.cloned.1.call-start
  45.9 0.0 copy-done.3
  45.9 0.0 copy-done
  45.9 6.0 %gather_fusion.2 = bf16[24,256,1024]{2,1,0:T(8,128)(2,1)} fusion(bf16[4,256,1024]{2,1,0:T(8,128)(2,1)S(1)} %bitcast.22, s32[1024]{0:T(1024)S(1)} %pad_clamp_fusion.2), kind=kCustom, calls=%fused_computation.clone | custom fusion | bytes 25165920 | tf_op jit(solution)/shard_map/jit(_take)/gather | solution.py:29
  51.9 7.8 %gather_fusion.3 = bf16[24,256,1024]{2,1,0:T(8,128)(2,1)} fusion(bf16[4,256,1024]{2,1,0:T(8,128)(2,1)} %bitcast.23, s32[1024]{0:T(1024)S(1)} %pad_clamp_fusion.2), kind=kCustom, calls=%fused_computation.1.clone | custom fusion | bytes 25165920 | tf_op jit(solution)/shard_map/jit(_take)/gather | solution.py:30
  59.7 83.6 %all-to-all-done = bf16[16,256,1024]{2,1,0:T(8,128)(2,1)} async-done(((bf16[16,256,1024]{2,1,0:T(8,128)(2,1)}), bf16[16,256,1024]{2,1,0:T(8,128)(2,1)}, u32[]{:S(2)}, u32[]{:S(2)}) %all-to-all-start) | async-done | bytes 8388640 | tf_op jit(solution)/shard_map/all_to_all | solution.py:21
  143.4 0.0 copy-done.2
  143.4 8.6 %pad_maximum_fusion.1 = bf16[20,256,1024]{2,1,0:T(8,128)(2,1)} fusion(bf16[16,256,1024]{2,1,0:T(8,128)(2,1)} %all-to-all-done, bf16[4,256,1024]{2,1,0:T(8,128)(2,1)S(1)} %bitcast.25), kind=kLoop, calls=%fused_computation.12 | loop fusion | flops 5242880 | bytes 20971520 | tf_op jit(solution)/shard_map/concatenate | solution.py:22
  152.0 10.1 %gather_fusion.1 = bf16[24,256,1024]{2,1,0:T(8,128)(2,1)} fusion(bf16[20,256,1024]{2,1,0:T(8,128)(2,1)} %pad_maximum_fusion.1, s32[1024]{0:T(1024)S(1)} %pad_clamp_fusion), kind=kCustom, calls=%fused_computation.3 | custom fusion | bytes 25165920 | tf_op jit(solution)/shard_map/jit(_take)/gather | solution.py:31
  162.1 13.1 %fusion.8 = f32[1,24,256,256]{3,2,1,0:T(8,128)} fusion(bf16[24,256,1024]{2,1,0:T(8,128)(2,1)} %gather_fusion.1, pred[24]{0:T(512)(128)(4,1)S(1)} %get-tuple-element.8, bf16[24,256,1024]{2,1,0:T(8,128)(2,1)} %gather_fusion.2, pred[24]{0:T(512)(128)(4,1)S(1)} %get-tuple-element.6), kind=kOutput, calls=%fused_computation.16 | convolution fusion | flops 3233808384 | bytes 31457328 | tf_op jit(solution)/shard_map/tak,tbk->tab/dot_general | solution.py:32
  175.1 13.0 %fusion.11 = f32[1,24,256,256]{3,2,1,0:T(8,128)} fusion(bf16[24,256,1024]{2,1,0:T(8,128)(2,1)} %gather_fusion.1, pred[24]{0:T(512)(128)(4,1)S(1)} %get-tuple-element.8, bf16[24,256,1024]{2,1,0:T(8,128)(2,1)} %gather_fusion.3, pred[24]{0:T(512)(128)(4,1)S(1)} %get-tuple-element.6), kind=kOutput, calls=%fused_computation.17 | convolution fusion | flops 3233808384 | bytes 31457328 | tf_op jit(solution)/shard_map/tak,tbk->tab/dot_general | solution.py:33
  188.2 10.7 %pad_maximum_fusion = f32[2,24,256,256]{3,2,1,0:T(8,128)} fusion(f32[1,24,256,256]{3,2,1,0:T(8,128)} %fusion.11, f32[1,24,256,256]{3,2,1,0:T(8,128)} %fusion.8), kind=kLoop, calls=%fused_computation.4 | loop fusion | flops 3145728 | bytes 25165824 | tf_op jit(solution)/shard_map/stack | solution.py:34
  198.9 0.0 all-reduce.2.cloned.1.call-update
  198.9 150.7 %all-reduce.2.cloned.1.call-done = f32[2,24,256,256]{3,2,1,0:T(8,128)} async-done(((f32[2,24,256,256]{3,2,1,0:T(8,128)}), f32[2,24,256,256]{3,2,1,0:T(8,128)}) %all-reduce.2.cloned.1.call-update) | async-done | bytes 12582928 | tf_op jit(solution)/shard_map/psum | solution.py:35
  349.6 2.4 fusion.14
  352.0 0.0 copy-done.1
  (12 shorter events, 0.1 us)
Async XLA Ops:
  6.5 39.4 %copy-start = (bf16[1024,1024]{1,0:T(8,128)(2,1)S(1)}, bf16[1024,1024]{1,0:T(8,128)(2,1)}, u32[]{:S(2)}) copy-start(bf16[1024,1024]{1,0:T(8,128)(2,1)} %param.6) | copy-start | bytes 6291460
  40.9 5.0 %copy-start.3 = (s32[24,2]{0,1:T(2,128)S(1)}, s32[24,2]{0,1:T(2,128)}, u32[]{:S(2)}) copy-start(s32[24,2]{0,1:T(2,128)} %param.9) | copy-start | bytes 580
  40.9 102.5 %all-to-all-start = ((bf16[16,256,1024]{2,1,0:T(8,128)(2,1)}), bf16[16,256,1024]{2,1,0:T(8,128)(2,1)}, u32[]{:S(2)}, u32[]{:S(2)}) async-start(bf16[16,256,1024]{2,1,0:T(8,128)(2,1)} %broadcast_select_fusion.1), calls=%async_computation | async-start | bytes 16777216 | tf_op jit(solution)/shard_map/all_to_all | solution.py:21
  45.8 303.8 %all-reduce.2.cloned.1.call-start = ((), (), s32[]{:S(2)}) async-start(), calls=%async_computation.1 | async-start | bytes 25165824 | tf_op jit(solution)/shard_map/psum | solution.py:35
  51.9 91.5 %copy-start.2 = (bf16[1024,1024]{1,0:T(8,128)(2,1)S(1)}, bf16[1024,1024]{1,0:T(8,128)(2,1)}, u32[]{:S(2)}) copy-start(bf16[1024,1024]{1,0:T(8,128)(2,1)} %param.8) | copy-start | bytes 6291460
  188.2 163.8 %copy-start.1 = (bf16[1024,1024]{1,0:T(8,128)(2,1)S(1)}, bf16[1024,1024]{1,0:T(8,128)(2,1)}, u32[]{:S(2)}) copy-start(bf16[1024,1024]{1,0:T(8,128)(2,1)} %param.6) | copy-start | bytes 6291460
Sparse Core Ops, SparseCore 0:
  199.1 150.5 all-reduce.1
where the time goes:
time: 359 us
  waiting for transfers between devices  234 us (65%)
  local copies, waits for them, and re-layouts  30.3 us (8%)
  other arithmetic  29.4 us (8%)
  matrix products  26.1 us (7%)
  blocking collectives  20.3 us (6%)
  between operations  13.5 us (4%)
  starting transfers between devices  4.98 us (1%)
    psum x1, waiting for transfers between devices, shards(): whole = lax.psum(stacked, 'col')  151 us
    all_to_all x1, waiting for transfers between devices, shards(): lax.all_to_all(outgoing, 'row', split_axis=0, concat_axis=0, tiled=True)  83.6 us
    all_gather x1, blocking collectives, shards(): every_pair = lax.all_gather(pairs, 'row', axis=0, tiled=True)  20.3 us
    dot_general x1, matrix products, shards(): jnp.einsum('tak,tbk->tab', left_x, right_rows, preferred_element_type=jnp...  13.1 us
    dot_general x1, matrix products, shards(): jnp.einsum('tak,tbk->tab', left_s, right_rows, preferred_element_type=jnp...  13 us
    another operation x1, other arithmetic, shards(): stacked = jnp.stack([cross_x, cross_s])  10.7 us
    gather x1, local copies, waits for them, and re-layouts, shards(): right_rows = jnp.take(block_table, second_slot, axis=0)  10.1 us
    concatenate x1, other arithmetic, shards(): block_table = jnp.concatenate([weight_blocks, incoming], axis=0)  8.62 us
  transfers between devices with their start and end apart: 2, of which 2 were waited for; matrix products, arithmetic and copies ran while one was open for 4% of the time, Pallas kernels for 0%

commit v1 on v0

--- a/solution.py
+++ b/solution.py
@@ -32,7 +32,11 @@
     cross_x = jnp.einsum("tak,tbk->tab", left_x, right_rows, preferred_element_type=jnp.float32)
     cross_s = jnp.einsum("tak,tbk->tab", left_s, right_rows, preferred_element_type=jnp.float32)
     stacked = jnp.stack([cross_x, cross_s])
-    whole = lax.psum(stacked, "col")
+    whole = stacked
+    wide_n = lax.psum(1, "col")
+    for jj in [dev_j for dev_j in (1, 2, 4, 8, 16) if dev_j < wide_n]:
+        outer = lax.ppermute(whole, "col", perm=tuple(((rr, rr ^ jj) for rr in range(wide_n))))
+        whole = whole + outer
     slice_rows = TILE // lax.axis_size("col")
     summed = lax.dynamic_slice_in_dim(whole, lax.axis_index("col") * slice_rows, slice_rows, 2)
     return summed[0] * summed[1]

time: 359 us -> 797 us (2.22)
  waiting for transfers between devices: 234 us -> 643 us
  other arithmetic: 29.4 us -> 58.5 us
  between operations: 13.5 us -> 0.13 us
  starting transfers between devices: 4.98 us -> 17.4 us
    ppermute x0 -> x3, waiting for transfers between devices: none -> 559 us  [shards(): lax.ppermute(whole, 'col', perm=tuple(((rr, rr ^ jj) for rr in range(wide...]
    psum x1 -> x0, waiting for transfers between devices: 151 us -> none  [shards(): whole = lax.psum(stacked, 'col')]
    add x0 -> x3, other arithmetic: none -> 30.6 us  [shards(): whole = whole + outer]
    ppermute x0 -> x3, starting transfers between devices: none -> 12.5 us  [shards(): lax.ppermute(whole, 'col', perm=tuple(((rr, rr ^ jj) for rr in range(wide...]
  transfers between devices with their start and end apart: 2 -> 4, of which waited for: 2 -> 4; matrix products, arithmetic and copies ran while one was open for 4% -> 2% of each run, Pallas kernels for 0% -> 0%
where the time goes in v1:
time: 797 us; the launch traced here: 796 us
  waiting for transfers between devices  643 us (81%)
  other arithmetic  58.5 us (7%)
  local copies, waits for them, and re-layouts  30.3 us (4%)
  matrix products  26.1 us (3%)
  blocking collectives  20.3 us (3%)
  starting transfers between devices  17.4 us (2%)
    ppermute x3, waiting for transfers between devices, shards(): lax.ppermute(whole, 'col', perm=tuple(((rr, rr ^ jj) for rr in range(wide...  559 us
    all_to_all x1, waiting for transfers between devices, shards(): lax.all_to_all(outgoing, 'row', split_axis=0, concat_axis=0, tiled=True)  83.7 us
    add x3, other arithmetic, shards(): whole = whole + outer  30.6 us
    all_gather x1, blocking collectives, shards(): every_pair = lax.all_gather(pairs, 'row', axis=0, tiled=True)  20.3 us
  transfers between devices with their start and end apart: 4, of which 4 were waited for; matrix products, arithmetic and copies ran while one was open for 2% of the time, Pallas kernels for 0%

profile of v1, /device:TPU:1, one launch (start us, length us, event | category | flops | bytes accessed | tf_op | source)
XLA Modules:
  0.0 795.6 jit_solution(12211022205247524841)
XLA Ops:
  0.0 20.3 %all-gather = s32[16,24,2]{1,2,0:T(2,128)S(1)} all-gather(s32[1,24,2]{1,2,0:T(2,128)} %bitcast.28), channel_id=1, replica_groups=mesh['row'=16,'col'=8] {'row'}, dimensions={0}, use_global_device_ids=true | all-gather | bytes 3264 | tf_op jit(solution)/shard_map/all_gather | solution.py:15
  20.3 0.1 reshape.79
  20.5 0.1 reduce_max.20
  20.7 6.2 gather_fusion
  26.9 7.4 broadcast_select_fusion.1
  34.3 4.9 all-to-all-start
  39.3 6.0 gather_fusion.3
  45.3 7.8 gather_fusion.2
  53.1 83.7 %all-to-all-done = bf16[16,256,1024]{2,1,0:T(8,128)(2,1)} async-done(((bf16[16,256,1024]{2,1,0:T(8,128)(2,1)}), bf16[16,256,1024]{2,1,0:T(8,128)(2,1)}, u32[]{:S(2)}, u32[]{:S(2)}) %all-to-all-start) | async-done | bytes 8388640 | tf_op jit(solution)/shard_map/all_to_all | solution.py:21
  136.8 8.6 %pad_maximum_fusion.1 = bf16[20,256,1024]{2,1,0:T(8,128)(2,1)} fusion(bf16[16,256,1024]{2,1,0:T(8,128)(2,1)} %all-to-all-done, bf16[4,256,1024]{2,1,0:T(8,128)(2,1)S(1)} %bitcast.27), kind=kLoop, calls=%fused_computation.12 | loop fusion | flops 5242880 | bytes 20971520 | tf_op jit(solution)/shard_map/concatenate | solution.py:22
  145.4 10.1 %gather_fusion.1 = bf16[24,256,1024]{2,1,0:T(8,128)(2,1)} fusion(bf16[20,256,1024]{2,1,0:T(8,128)(2,1)} %pad_maximum_fusion.1, s32[1024]{0:T(1024)S(1)} %pad_clamp_fusion), kind=kCustom, calls=%fused_computation.3 | custom fusion | bytes 25165920 | tf_op jit(solution)/shard_map/jit(_take)/gather | solution.py:31
  155.5 13.1 %fusion.11 = f32[1,24,256,256]{3,2,1,0:T(8,128)} fusion(bf16[24,256,1024]{2,1,0:T(8,128)(2,1)} %gather_fusion.1, pred[24]{0:T(512)(128)(4,1)S(1)} %get-tuple-element.8, bf16[24,256,1024]{2,1,0:T(8,128)(2,1)} %gather_fusion.3, pred[24]{0:T(512)(128)(4,1)S(1)} %get-tuple-element.6), kind=kOutput, calls=%fused_computation.17 | convolution fusion | flops 3233808384 | bytes 31457328 | tf_op jit(solution)/shard_map/tak,tbk->tab/dot_general | solution.py:33
  168.6 13.0 %fusion.8 = f32[1,24,256,256]{3,2,1,0:T(8,128)} fusion(bf16[24,256,1024]{2,1,0:T(8,128)(2,1)} %gather_fusion.1, pred[24]{0:T(512)(128)(4,1)S(1)} %get-tuple-element.8, bf16[24,256,1024]{2,1,0:T(8,128)(2,1)} %gather_fusion.2, pred[24]{0:T(512)(128)(4,1)S(1)} %get-tuple-element.6), kind=kOutput, calls=%fused_computation.16 | convolution fusion | flops 3233808384 | bytes 31457328 | tf_op jit(solution)/shard_map/tak,tbk->tab/dot_general | solution.py:32
  181.6 10.6 %pad_maximum_fusion = f32[2,24,256,256]{3,2,1,0:T(8,128)} fusion(f32[1,24,256,256]{3,2,1,0:T(8,128)} %fusion.11, f32[1,24,256,256]{3,2,1,0:T(8,128)} %fusion.8), kind=kLoop, calls=%fused_computation.4 | loop fusion | flops 3145728 | bytes 25165824 | tf_op jit(solution)/shard_map/stack | solution.py:34
  192.2 8.3 %collective-permute-start = (f32[2,24,256,256]{3,2,1,0:T(8,128)}, f32[2,24,256,256]{3,2,1,0:T(8,128)}, u32[]{:S(2)}, u32[]{:S(2)}) collective-permute-start(f32[2,24,256,256]{3,2,1,0:T(8,128)} %pad_maximum_fusion), channel_id=1, source_target_pairs={{0,1},{1,0},{2,3},{3,2},{4,5},{5,4},{6,7},{7,6},{8,9},{9,8},{10,11... | collective-permute-start | bytes 37748744 | tf_op jit(solution)/shard_map/ppermute | solution.py:38
  200.6 19.1 %collective-permute-done = f32[2,24,256,256]{3,2,1,0:T(8,128)} collective-permute-done((f32[2,24,256,256]{3,2,1,0:T(8,128)}, f32[2,24,256,256]{3,2,1,0:T(8,128)}, u32[]{:S(2)}, u32[]{:S(2)}) %collective-permute-start) | collective-permute-done | bytes 12582944 | tf_op jit(solution)/shard_map/ppermute | solution.py:38
  219.7 14.1 %fusion.19 = f32[2,24,256,256]{3,2,1,0:T(8,128)} fusion(f32[2,24,256,256]{3,2,1,0:T(8,128)} %collective-permute-done, f32[1,24,256,256]{3,2,1,0:T(8,128)} %fusion.11, f32[1,24,256,256]{3,2,1,0:T(8,128)} %fusion.8), kind=kLoop, calls=%fused_computation.45 | loop fusion | flops 6291456 | bytes 37748736 | tf_op jit(solution)/shard_map/add | solution.py:39
  233.7 1.3 collective-permute-start.1
  235.0 270.5 %collective-permute-done.1 = f32[2,24,256,256]{3,2,1,0:T(8,128)} collective-permute-done((f32[2,24,256,256]{3,2,1,0:T(8,128)}, f32[2,24,256,256]{3,2,1,0:T(8,128)}, u32[]{:S(2)}, u32[]{:S(2)}) %collective-permute-start.1) | collective-permute-done | bytes 12582944 | tf_op jit(solution)/shard_map/ppermute | solution.py:38
  505.6 14.4 %fusion.20 = f32[2,24,256,256]{3,2,1,0:T(8,128)} fusion(f32[2,24,256,256]{3,2,1,0:T(8,128)} %collective-permute-done.1, f32[2,24,256,256]{3,2,1,0:T(8,128)} %collective-permute-done, f32[1,24,256,256]{3,2,1,0:T(8,128)S(1)} %bitcast.25, f32[1,24,256,256]{3,2,1,0:T(8,128)S(1)} %copy-done.2), kind=kLoop, calls=%fused_computation.46 | loop fusion | flops 9437184 | bytes 50331648 | tf_op jit(solution)/shard_map/add | solution.py:39
  520.0 2.9 collective-permute-start.2
  522.9 269.6 %collective-permute-done.2 = f32[2,24,256,256]{3,2,1,0:T(8,128)} collective-permute-done((f32[2,24,256,256]{3,2,1,0:T(8,128)}, f32[2,24,256,256]{3,2,1,0:T(8,128)}, u32[]{:S(2)}, u32[]{:S(2)}) %collective-permute-start.2) | collective-permute-done | bytes 12582944 | tf_op jit(solution)/shard_map/ppermute | solution.py:38
  792.5 2.2 dynamic-slice_add_fusion
  794.6 1.0 fusion.14
  (25 shorter events, 0.2 us)
Async XLA Ops:
  0.0 39.3 %copy-start = (bf16[1024,1024]{1,0:T(8,128)(2,1)S(1)}, bf16[1024,1024]{1,0:T(8,128)(2,1)}, u32[]{:S(2)}) copy-start(bf16[1024,1024]{1,0:T(8,128)(2,1)} %param.7) | copy-start | bytes 6291460
  34.3 4.9 copy-start.4
  34.3 102.4 %all-to-all-start = ((bf16[16,256,1024]{2,1,0:T(8,128)(2,1)}), bf16[16,256,1024]{2,1,0:T(8,128)(2,1)}, u32[]{:S(2)}, u32[]{:S(2)}) async-start(bf16[16,256,1024]{2,1,0:T(8,128)(2,1)} %broadcast_select_fusion.1), calls=%async_computation | async-start | bytes 16777216 | tf_op jit(solution)/shard_map/all_to_all | solution.py:21
  45.3 91.5 %copy-start.3 = (bf16[1024,1024]{1,0:T(8,128)(2,1)S(1)}, bf16[1024,1024]{1,0:T(8,128)(2,1)}, u32[]{:S(2)}) copy-start(bf16[1024,1024]{1,0:T(8,128)(2,1)} %param.8) | copy-start | bytes 6291460
  181.6 324.0 %slice-start = ((s8[6291456]{0:T(1024)(128)(4,1)}), s8[2097152]{0:T(1024)(128)(4,1)S(1)}, s32[]{:S(2)}) async-start(s8[6291456]{0:T(1024)(128)(4,1)} %bitcast.24), calls=%async_computation.1 | async-start | bytes 4194304
  192.2 313.3 %slice-start.1 = ((s8[6291456]{0:T(1024)(128)(4,1)}), s8[4194304]{0:T(1024)(128)(4,1)S(1)}, s32[]{:S(2)}) async-start(s8[6291456]{0:T(1024)(128)(4,1)} %bitcast.24), calls=%async_computation.2 | async-start | bytes 8388608
  192.2 313.3 %copy-start.2 = (f32[1,24,256,256]{3,2,1,0:T(8,128)S(1)}, f32[1,24,256,256]{3,2,1,0:T(8,128)}, u32[]{:S(2)}) copy-start(f32[1,24,256,256]{3,2,1,0:T(8,128)} %fusion.8) | copy-start | bytes 18874372
  192.2 27.4 %collective-permute-start = (f32[2,24,256,256]{3,2,1,0:T(8,128)}, f32[2,24,256,256]{3,2,1,0:T(8,128)}, u32[]{:S(2)}, u32[]{:S(2)}) collective-permute-start(f32[2,24,256,256]{3,2,1,0:T(8,128)} %pad_maximum_fusion), channel_id=1, source_target_pairs={{0,1},{1,0},{2,3},{3,2},{4,5},{5,4},{6,7},{7,6},{8,9},{9,8},{10,11... | collective-permute-start | bytes 37748744 | tf_op jit(solution)/shard_map/ppermute | solution.py:38
  233.7 271.8 %collective-permute-start.1 = (f32[2,24,256,256]{3,2,1,0:T(8,128)}, f32[2,24,256,256]{3,2,1,0:T(8,128)}, u32[]{:S(2)}, u32[]{:S(2)}) collective-permute-start(f32[2,24,256,256]{3,2,1,0:T(8,128)} %fusion.19), channel_id=1, source_target_pairs={{0,2},{1,3},{2,0},{3,1},{4,6},{5,7},{6,4},{7,5},{8,10},{9,11},{10,... | collective-permute-start | bytes 37748744 | tf_op jit(solution)/shard_map/ppermute | solution.py:38
  505.6 290.0 %copy-start.1 = (bf16[1024,1024]{1,0:T(8,128)(2,1)S(1)}, bf16[1024,1024]{1,0:T(8,128)(2,1)}, u32[]{:S(2)}) copy-start(bf16[1024,1024]{1,0:T(8,128)(2,1)} %param.7) | copy-start | bytes 6291460
  520.0 272.5 %collective-permute-start.2 = (f32[2,24,256,256]{3,2,1,0:T(8,128)}, f32[2,24,256,256]{3,2,1,0:T(8,128)}, u32[]{:S(2)}, u32[]{:S(2)}) collective-permute-start(f32[2,24,256,256]{3,2,1,0:T(8,128)} %fusion.20), channel_id=1, source_target_pairs={{0,4},{1,5},{2,6},{3,7},{4,0},{5,1},{6,2},{7,3},{8,12},{9,13},{10,... | collective-permute-start | bytes 37748744 | tf_op jit(solution)/shard_map/ppermute | solution.py:38
